TPU v7x, 32 devices: a whole 2x2x4 slice. The times are simulated.
32 devices in a mesh: rep: 4 (over y, x), fsdp: 8 (over z, core).
Axes of the slice: x: 2, y: 2, z: 4, core: 2. Of those that a mesh axis runs over, the one named last changes fastest.
Arguments:
- tokens: bfloat16 [6144, 4096], P(('rep', 'fsdp')), may hold values from -6 to 6
- cotangent: bfloat16 [6144, 256], P(('rep', 'fsdp')), may hold values from -6 to 6
- weight: float32 [4096, 256], P('fsdp'), may hold values from -0.09375 to 0.09375
- momentum: float32 [4, 4096, 256], P('rep', 'fsdp'), may hold values from -6 to 6
- column_order: int32 [64], replicated, may hold values from 0 to 63, each once
Outputs:
- input_grad: bfloat16 [6144, 4096], P(('rep', 'fsdp'))
- new_momentum: float32 [4, 4096, 256], P('rep', 'fsdp')
- update: float32 [4096, 256], P('fsdp')
- new_weight: float32 [4096, 256], P('fsdp')
Inputs may be any that keep to these rules, and one draw needn't show every extreme that they name: `column_order`: each of the 64 frequency indices appears exactly once.
All inputs are finite; a program needn't handle non-finite values.
Results may differ from a plain program's by a relative error of at most 0.0049.
Values may be sent and summed in bfloat16 or wider, within the bound.
No kernel may reach another device: no remote copies, remote signals or barrier semaphores. Data moves between devices by JAX's collectives and lax.ppermute only.
A program may use at most 64 MiB of HBM per device.

v0:
```python
import math
import jax
import jax.numpy as jnp
from jax import lax
from jax.sharding import PartitionSpec as P

KW = 256
BLOCK = 64
SEL = 16
MOMENTUM_DECAY = 0.9
LEARN_RATE = 0.05


def dct_table():
    index = jnp.arange(BLOCK).astype(jnp.float32)
    table = jnp.cos(
        math.pi * (2.0 * index[None, :] + 1.0) * index[:, None] / (2.0 * BLOCK)
    ) * math.sqrt(2.0 / BLOCK)
    return jnp.where(index[:, None] == 0.0, table * math.sqrt(0.5), table)


def on_device(tokens, cotangent, weight, momentum, column_order):
    members = lax.axis_size("fsdp")
    replicas = lax.axis_size("rep")
    rows_own = weight.shape[0]
    table = dct_table()
    weight_half = weight.astype(jnp.bfloat16)
    input_grad = lax.dot_general(
        cotangent,
        lax.all_gather(weight_half, "fsdp", axis=0, tiled=True),
        (((1,), (1,)), ((), ())),
        preferred_element_type=jnp.float32,
    ).astype(jnp.bfloat16)
    scale = float(tokens.shape[0] * members) ** (-0.5)
    weight_grad = (
        lax.psum_scatter(
            lax.dot_general(
                tokens, cotangent, (((0,), (0,)), ((), ())), preferred_element_type=jnp.float32
            ),
            "fsdp",
            scatter_dimension=0,
            tiled=True,
        )
        * scale
    )
    moment = MOMENTUM_DECAY * momentum[0] + weight_grad
    blocks = moment.reshape(rows_own // BLOCK, BLOCK, KW // BLOCK, BLOCK)
    coeffs = jnp.einsum("kn,anbm,lm->akbl", table, blocks, table, precision=lax.Precision.HIGHEST)
    picker = (jnp.arange(BLOCK)[:, None] == column_order[None, :SEL]).astype(jnp.float32)
    compact = jnp.einsum("akbl,ls->akbs", coeffs, picker, precision=lax.Precision.HIGHEST)
    sent = jnp.einsum("akbs,ls->akbl", compact, picker, precision=lax.Precision.HIGHEST)
    own_back = jnp.einsum("kn,akbl,lm->anbm", table, sent, table, precision=lax.Precision.HIGHEST)
    new_momentum = (moment - own_back.reshape(rows_own, KW))[None]
    flat_sent = compact.reshape(-1)
    gathered = lax.all_gather(flat_sent, "rep", axis=0, tiled=True)
    summed = jnp.sum(gathered.reshape(replicas, -1), axis=0)
    summed_full = jnp.einsum(
        "akbs,ls->akbl", summed.reshape(compact.shape), picker, precision=lax.Precision.HIGHEST
    )
    decoded = jnp.einsum(
        "kn,akbl,lm->anbm", table, summed_full, table, precision=lax.Precision.HIGHEST
    )
    update = decoded.reshape(rows_own, KW) / replicas
    new_weight = weight - LEARN_RATE * update
    return (input_grad, new_momentum, update, new_weight)


def solution(mesh):
    in_specs = (
        P(("rep", "fsdp"), None),
        P(("rep", "fsdp"), None),
        P("fsdp", None),
        P("rep", "fsdp", None),
        P(),
    )
    out_specs = (P(("rep", "fsdp"), None), P("rep", "fsdp", None), P("fsdp", None), P("fsdp", None))
    return jax.shard_map(
        on_device, mesh=mesh, in_specs=in_specs, out_specs=out_specs, check_vma=False
    )
```

profile of v0, /device:TPU:0, one launch (start us, length us, event | category | flops | bytes accessed | tf_op | source)
XLA Modules:
  0.0 147.0 jit_solution(15613769380523077113)
XLA Ops:
  7.2 1.9 %convert_element_type.31 = bf16[512,256]{1,0:T(8,128)(2,1)} convert(f32[512,256]{1,0:T(8,128)} %param.7) | non-fusion elementwise | flops 131072 | bytes 786432 | tf_op jit(solution)/shard_map/convert_element_type | solution.py:27
  9.2 3.6 %fusion.78 = f32[4096,256]{1,0:T(8,128)} fusion(bf16[192,4096]{1,0:T(8,128)(2,1)S(1)} %copy-done, bf16[192,256]{1,0:T(8,128)(2,1)} %param.6), kind=kOutput, calls=%fused_computation.85 | convolution fusion | flops 402653184 | bytes 5865472 | tf_op jit(solution)/shard_map/dot_general | solution.py:37
  12.8 1.0 copy-done.2
  13.8 1.0 copy.42
  14.9 27.2 %all-gather.2.cloned.1.call-done = bf16[4096,256]{1,0:T(8,128)(2,1)} async-done(((bf16[512,256]{1,0:T(8,128)(2,1)}), bf16[4096,256]{1,0:T(8,128)(2,1)}) %all-gather.2.cloned.1.call-update) | async-done | bytes 2097168 | tf_op jit(solution)/shard_map/all_gather | solution.py:30
  42.1 3.6 %convolution_convert_fusion = bf16[192,4096]{1,0:T(8,128)(2,1)} fusion(bf16[192,256]{1,0:T(8,128)(2,1)S(1)} %copy-done.4, bf16[4096,256]{1,0:T(8,128)(2,1)} %all-gather.2.cloned.1.call-done), kind=kOutput, calls=%fused_computation | convolution fusion | flops 403439616 | bytes 3768320 | tf_op jit(solution)/shard_map/dot_general | solution.py:28
  45.6 48.1 %reduce-scatter.2.cloned.1.call-done = f32[512,256]{1,0:T(8,128)} async-done(((f32[4096,256]{1,0:T(8,128)}), f32[512,256]{1,0:T(8,128)}) %reduce-scatter.2.cloned.1.call-update) | async-done | bytes 524304 | tf_op jit(solution)/shard_map/reduce_scatter | solution.py:36
  93.7 1.1 bitcast_add_fusion
  94.8 0.5 reshape.49
  95.3 1.3 fusion.2
  96.6 1.1 convolution_bitcast_fusion.1
  97.8 1.3 fusion.53
  99.1 0.4 copy.36
  99.5 1.7 %fusion.51 = f32[8,64,4,64]{1,3,2,0:T(8,128)} fusion(f32[8,64,4,16]{1,3,2,0:T(8,128)S(1)} %fusion.53, s32[16]{0:T(128)S(1)} %bitcast.53), kind=kOutput, calls=%fused_computation.59 | convolution fusion | flops 25166848 | bytes 655424 | tf_op jit(solution)/shard_map/akbs,ls->akbl/dot_general | solution.py:51
  101.2 0.7 reshape.51
  101.8 10.9 %all_gather.7 = f32[131072]{0:T(1024)S(1)} all-gather(f32[32768]{0:T(1024)S(1)} %reshape.51), channel_id=1, replica_groups=mesh['rep'=4,'fsdp'=8] {'rep'}, dimensions={0}, use_global_device_ids=true | all-gather | bytes 655360 | tf_op jit(solution)/shard_map/all_gather | solution.py:55
  113.0 0.3 reduce_sum.9
  113.3 0.7 reshape.53
  114.0 1.7 %fusion = f32[8,64,4,64]{1,3,2,0:T(8,128)S(1)} fusion(f32[8,64,4,16]{3,2,1,0:T(4,128)S(1)} %reshape.53, s32[16]{0:T(128)S(1)} %bitcast.54), kind=kOutput, calls=%fused_computation.3 | convolution fusion | flops 25166848 | bytes 655424 | tf_op jit(solution)/shard_map/akbs,ls->akbl/dot_general | solution.py:57
  115.7 3.3 %fusion.6 = f32[8,4,64,64]{2,3,1,0:T(8,128)S(1)} fusion(f32[8,64,4,64]{1,3,2,0:T(8,128)S(1)} %fusion, f32[64]{0:T(128)S(1)} %iota_convert_fusion, f32[64]{0:T(128)S(1)} %add_multiply_fusion, pred[64]{0:T(512)(128)(4,1)S(1)} %broadcast_compare_fusion), kind=kOutput, calls=%fused_computation.13 | convolution fusion | flops 100683776 | bytes 1049152 | tf_op jit(solution)/shard_map/kn,akbl,lm->anbm/dot_general | solution.py:60
  119.0 2.2 %multiply_bitcast_fusion = (f32[8,64,4,64]{3,1,2,0:T(8,128)S(1)}, f32[8,64,4,64]{3,1,2,0:T(8,128)}) fusion(f32[8,4,64,64]{2,3,1,0:T(8,128)S(1)} %fusion.6, f32[64]{0:T(128)S(1)} %iota_convert_fusion, f32[64]{0:T(128)S(1)} %add_multiply_fusion, pred[64]{0:T(512)(128)(4,1)S(1)} %broadcast_compare_fusion), kind=kOutput, calls=%fused_computation.7 | convolution fusion | flops 100945920 | bytes 1573440 | tf_op jit(solution)/shard_map/kn,akbl,lm->anbm/dot_general | solution.py:60
  121.2 1.3 copy.41
  122.5 1.5 %mul.163 = f32[512,256]{0,1:T(8,128)S(1)} reshape(f32[8,64,4,64]{1,0,3,2:T(8,128)} %copy.41) | data formatting | bytes 1048576 | tf_op jit(solution)/shard_map/mul | solution.py:64
  124.0 1.1 sub.7
  125.1 1.0 copy.44
  126.1 3.0 %copy.52 = f32[8,64,4,64]{3,2,1,0:T(4,128)} copy(f32[8,64,4,64]{3,1,2,0:T(8,128)} %get-tuple-element.17) | data formatting | bytes 1048576
  129.1 2.6 %reshape.56 = f32[512,256]{1,0:T(8,128)} reshape(f32[8,64,4,64]{3,2,1,0:T(4,128)} %copy.52) | data formatting | bytes 1048576
  131.7 3.3 %fusion.9 = f32[8,4,64,64]{2,3,1,0:T(8,128)S(1)} fusion(f32[8,64,4,64]{1,3,2,0:T(8,128)S(1)} %copy-done.1, f32[64]{0:T(128)S(1)} %iota_convert_fusion, f32[64]{0:T(128)S(1)} %add_multiply_fusion, pred[64]{0:T(512)(128)(4,1)S(1)} %broadcast_compare_fusion), kind=kOutput, calls=%fused_computation.16 | convolution fusion | flops 100683776 | bytes 1049152 | tf_op jit(solution)/shard_map/kn,akbl,lm->anbm/dot_general | solution.py:52
  135.0 1.1 convolution_bitcast_fusion
  136.2 0.7 copy.35
  136.9 1.4 reshape.50
  138.3 1.9 %subtract_bitcast_fusion = f32[1,512,256]{2,1,0:T(8,128)} fusion(f32[512,256]{1,0:T(8,128)S(1)} %bitcast_add_fusion, f32[512,256]{1,0:T(8,128)} %reshape.50), kind=kLoop, calls=%fused_computation.10 | loop fusion | flops 131072 | bytes 1572864 | tf_op jit(solution)/shard_map/broadcast_in_dim | solution.py:53
  (19 shorter events, 0.4 us)
Async XLA Ops:
  7.2 2.0 %copy-start = (bf16[192,4096]{1,0:T(8,128)(2,1)S(1)}, bf16[192,4096]{1,0:T(8,128)(2,1)}, u32[]{:S(2)}) copy-start(bf16[192,4096]{1,0:T(8,128)(2,1)} %param.5) | copy-start | bytes 4718596
  7.2 34.9 %all-gather.2.cloned.1.call-start = ((), (), s32[]{:S(2)}) async-start(), calls=%async_computation.1 | async-start | bytes 2359296 | tf_op jit(solution)/shard_map/all_gather | solution.py:30
  9.1 84.6 %reduce-scatter.2.cloned.1.call-start = ((), (), s32[]{:S(2)}) async-start(), calls=%async_computation.2 | async-start | bytes 4718592 | tf_op jit(solution)/shard_map/reduce_scatter | solution.py:36
  12.8 1.0 copy-start.2
  12.8 29.3 %copy-start.4 = (bf16[192,256]{1,0:T(8,128)(2,1)S(1)}, bf16[192,256]{1,0:T(8,128)(2,1)}, u32[]{:S(2)}) copy-start(bf16[192,256]{1,0:T(8,128)(2,1)} %param.6) | copy-start | bytes 294916
  14.8 78.9 %copy-start.3 = (f32[1,512,256]{2,1,0:T(8,128)S(1)}, f32[1,512,256]{2,1,0:T(8,128)}, u32[]{:S(2)}) copy-start(f32[1,512,256]{2,1,0:T(8,128)} %param.8) | copy-start | bytes 1572868
  95.3 2.5 %copy-start.5 = (s32[64]{0:T(128)S(1)}, s32[64]{0:T(128)}, u32[]{:S(2)}) copy-start(s32[64]{0:T(128)} %param.9) | copy-start | bytes 772
  126.1 5.6 %copy-start.1 = (f32[8,64,4,64]{1,3,2,0:T(8,128)S(1)}, f32[8,64,4,64]{1,3,2,0:T(8,128)}, u32[]{:S(2)}) copy-start(f32[8,64,4,64]{1,3,2,0:T(8,128)} %fusion.51) | copy-start | bytes 1572868
Sparse Core Ops, SparseCore 0:
  10.2 31.8 all-gather.1
  44.4 49.3 reduce-scatter.1
where the time goes:
time: 147 us
  waiting for transfers between devices  75.3 us (51%)
  matrix products  24.2 us (16%)
  local copies, waits for them, and re-layouts  16 us (11%)
  between operations  14.2 us (10%)
  blocking collectives  10.9 us (7%)
  other arithmetic  6.36 us (4%)
    reduce_scatter x1, waiting for transfers between devices, on_device(): lax.psum_scatter(lax.dot_general(tokens, cotangent, (((0,), (0,)), ((), (...  48.1 us
    all_gather x1, waiting for transfers between devices, on_device(): lax.all_gather(weight_half, 'fsdp', axis=0, tiled=True)  27.2 us
    all_gather x1, blocking collectives, on_device(): gathered = lax.all_gather(flat_sent, 'rep', axis=0, tiled=True)  10.9 us
    unnamed x16, local copies, waits for them, and re-layouts  8.64 us
    dot_general x2, matrix products, on_device(): jnp.einsum('kn,akbl,lm->anbm', table, summed_full, table, precision=lax.P...  5.46 us
    dot_general x2, matrix products, on_device(): jnp.einsum('kn,akbl,lm->anbm', table, sent, table, precision=lax.Precisio...  4.42 us
    dot_general x1, matrix products, on_device(): lax.dot_general(tokens, cotangent, (((0,), (0,)), ((), ())), preferred_el...  3.61 us
    dot_general x1, matrix products, on_device(): lax.dot_general(cotangent, lax.all_gather(weight_half, 'fsdp', axis=0, ti...  3.58 us
  transfers between devices with their start and end apart: 2, of which 2 were waited for; matrix products, arithmetic and copies ran while one was open for 6% of the time, Pallas kernels for 0%

commit v1 on v0

--- a/solution.py
+++ b/solution.py
@@ -3,12 +3,40 @@
 import jax.numpy as jnp
 from jax import lax
 from jax.sharding import PartitionSpec as P
+from jax.lax import axis_index, ppermute, psum
 
 KW = 256
 BLOCK = 64
 SEL = 16
 MOMENTUM_DECAY = 0.9
 LEARN_RATE = 0.05
+
+
+def space_cut(t0, row_dim):
+    x_now = list(t0.shape[1:])
+    x_now[row_dim] *= t0.shape[0]
+    big = jnp.moveaxis(t0, 0, row_dim).reshape(x_now)
+    return big
+
+
+def supply_all_the_corner(tile_in, row_axis):
+    current_arr = tile_in[None]
+    k_all = psum(1, row_axis)
+    for idx in range(k_all.bit_length() - 1):
+        r_now = 1 << idx
+        pages = []
+        for kk in range(k_all):
+            pages.append((kk, kk ^ r_now))
+        low = ppermute(current_arr, axis_name=row_axis, perm=pages)
+        local_out = jnp.stack([current_arr, low])
+        g_now = axis_index(row_axis) >> idx & 1
+        current_arr = jnp.where(g_now == 0, local_out, local_out[::-1]).reshape(-1, *tile_in.shape)
+    return current_arr
+
+
+def _detail_grid(mat, xs, dim_i):
+    oldest = space_cut(supply_all_the_corner(mat, xs), dim_i)
+    return oldest
 
 
 def dct_table():
@@ -27,7 +55,7 @@
     weight_half = weight.astype(jnp.bfloat16)
     input_grad = lax.dot_general(
         cotangent,
-        lax.all_gather(weight_half, "fsdp", axis=0, tiled=True),
+        _detail_grid(weight_half, "fsdp", 0),
         (((1,), (1,)), ((), ())),
         preferred_element_type=jnp.float32,
     ).astype(jnp.bfloat16)

time: 147 us -> 174 us (1.18)
  waiting for transfers between devices: 75.3 us -> 91.2 us
  starting transfers between devices: 0.08 us -> 6.15 us
  local copies, waits for them, and re-layouts: 16 us -> 20.8 us
  other arithmetic: 6.36 us -> 8.83 us
    ppermute x0 -> x3, waiting for transfers between devices: none -> 91.2 us  [supply_all_the_corner(): low = ppermute(current_arr, axis_name=row_axis, perm=pages)]
    reduce_scatter x1, waiting for transfers between devices: 48.1 us -> 0.01 us  [on_device(): lax.psum_scatter(lax.dot_general(tokens, cotangent, (((0,), (0,)), ((), (...]
    all_gather x1 -> x0, waiting for transfers between devices: 27.2 us -> none  [on_device(): lax.all_gather(weight_half, 'fsdp', axis=0, tiled=True)]
    ppermute x0 -> x3, starting transfers between devices: none -> 6.11 us  [supply_all_the_corner(): low = ppermute(current_arr, axis_name=row_axis, perm=pages)]
    another operation x0 -> x5, other arithmetic: none -> 2.77 us  [supply_all_the_corner(): local_out = jnp.stack([current_arr, low])]
    convert_element_type x1 -> x0, other arithmetic: 1.88 us -> none  [on_device(): weight_half = weight.astype(jnp.bfloat16)]
    unnamed x16 -> x18, local copies, waits for them, and re-layouts: 8.64 us -> 10.2 us
  transfers between devices with their start and end apart: 2 -> 4, of which waited for: 2 -> 3; matrix products, arithmetic and copies ran while one was open for 6% -> 4% of each run, Pallas kernels for 0% -> 0%
where the time goes in v1:
time: 174 us
  waiting for transfers between devices  91.2 us (52%)
  matrix products  22.6 us (13%)
  local copies, waits for them, and re-layouts  20.8 us (12%)
  between operations  14.2 us (8%)
  blocking collectives  10.2 us (6%)
  other arithmetic  8.83 us (5%)
  starting transfers between devices  6.15 us (4%)
    ppermute x3, waiting for transfers between devices, supply_all_the_corner(): low = ppermute(current_arr, axis_name=row_axis, perm=pages)  91.2 us
    all_gather x1, blocking collectives, on_device(): gathered = lax.all_gather(flat_sent, 'rep', axis=0, tiled=True)  10.2 us
    unnamed x18, local copies, waits for them, and re-layouts  10.2 us
    ppermute x3, starting transfers between devices, supply_all_the_corner(): low = ppermute(current_arr, axis_name=row_axis, perm=pages)  6.11 us
    dot_general x2, matrix products, on_device(): jnp.einsum('kn,akbl,lm->anbm', table, summed_full, table, precision=lax.P...  5.41 us
    dot_general x2, matrix products, on_device(): jnp.einsum('kn,akbl,lm->anbm', table, sent, table, precision=lax.Precisio...  4.42 us
    mul x2, local copies, waits for them, and re-layouts, on_device(): new_weight = weight - LEARN_RATE * update  3.7 us
    dot_general x1, matrix products, on_device(): lax.dot_general(tokens, cotangent, (((0,), (0,)), ((), ())), preferred_el...  3.62 us
  transfers between devices with their start and end apart: 4, of which 3 were waited for; matrix products, arithmetic and copies ran while one was open for 4% of the time, Pallas kernels for 0%

profile of v1, /device:TPU:0, one launch (start us, length us, event | category | flops | bytes accessed | tf_op | source)
XLA Modules:
  0.0 173.9 jit_solution(7560440732032471648)
XLA Ops:
  7.2 1.4 copy-done
  8.6 3.6 %fusion.81 = f32[4096,256]{1,0:T(8,128)} fusion(bf16[192,4096]{1,0:T(8,128)(2,1)S(1)} %copy-done, bf16[192,256]{1,0:T(8,128)(2,1)} %param.6), kind=kOutput, calls=%fused_computation.96 | convolution fusion | flops 402653184 | bytes 5865472 | tf_op jit(solution)/shard_map/dot_general | solution.py:65
  12.2 1.0 copy-done.3
  13.8 1.2 collective-permute-done
  15.2 3.0 %collective-permute-start.1 = (bf16[2,512,256]{2,1,0:T(8,128)(2,1)S(1)}, bf16[2,512,256]{2,1,0:T(8,128)(2,1)}, u32[]{:S(2)}, u32[]{:S(2)}) collective-permute-start(bf16[2,512,256]{2,1,0:T(8,128)(2,1)S(1)} %get-tuple-element.19), channel_id=1, source_target_pairs={{0,2},{1,3},{2,0},{3,1},{4,6},{5,7},{6,4},{7,5},{8,10},{9,11},{10,... | collective-permute-start | bytes 1572872 | tf_op jit(solution)/shard_map/ppermute | solution.py:30
  18.2 21.1 %collective-permute-done.1 = bf16[2,512,256]{2,1,0:T(8,128)(2,1)} collective-permute-done((bf16[2,512,256]{2,1,0:T(8,128)(2,1)S(1)}, bf16[2,512,256]{2,1,0:T(8,128)(2,1)}, u32[]{:S(2)}, u32[]{:S(2)}) %collective-permute-start.1) | collective-permute-done | bytes 524320 | tf_op jit(solution)/shard_map/ppermute | solution.py:30
  39.2 1.1 pad_maximum_fusion.1
  40.6 2.6 %collective-permute-start.2 = (bf16[4,512,256]{2,1,0:T(8,128)(2,1)S(1)}, bf16[4,512,256]{2,1,0:T(8,128)(2,1)}, u32[]{:S(2)}, u32[]{:S(2)}) collective-permute-start(bf16[4,512,256]{2,1,0:T(8,128)(2,1)S(1)} %bitcast.69), channel_id=1, source_target_pairs={{0,4},{1,5},{2,6},{3,7},{4,0},{5,1},{6,2},{7,3},{8,12},{9,13},{10,... | collective-permute-start | bytes 3145736 | tf_op jit(solution)/shard_map/ppermute | solution.py:30
  43.2 1.0 copy.42
  44.2 68.9 %collective-permute-done.2 = bf16[4,512,256]{2,1,0:T(8,128)(2,1)} collective-permute-done((bf16[4,512,256]{2,1,0:T(8,128)(2,1)S(1)}, bf16[4,512,256]{2,1,0:T(8,128)(2,1)}, u32[]{:S(2)}, u32[]{:S(2)}) %collective-permute-start.2) | collective-permute-done | bytes 1048608 | tf_op jit(solution)/shard_map/ppermute | solution.py:30
  113.1 1.4 pad_maximum_fusion
  115.4 2.0 %fusion = bf16[192,4096]{1,0:T(8,128)(2,1)} fusion(bf16[4096,256]{1,0:T(8,128)(2,1)S(1)} %bitcast.68, bf16[192,256]{1,0:T(8,128)(2,1)S(1)} %copy-done.5), kind=kOutput, calls=%fused_computation.1 | convolution fusion | flops 403439616 | bytes 3768320 | tf_op jit(solution)/shard_map/dot_general | solution.py:56
  117.4 1.1 bitcast_add_fusion
  119.0 1.3 fusion.3
  120.3 1.1 convolution_bitcast_fusion.1
  121.5 1.3 fusion.56
  123.2 1.7 fusion.54
  125.6 10.2 %all_gather.3 = f32[131072]{0:T(1024)S(1)} all-gather(f32[32768]{0:T(1024)S(1)} %reshape.59), channel_id=1, replica_groups=mesh['rep'=4,'fsdp'=8] {'rep'}, dimensions={0}, use_global_device_ids=true | all-gather | bytes 655360 | tf_op jit(solution)/shard_map/all_gather | solution.py:83
  137.0 1.7 fusion.1
  138.7 3.3 %fusion.9 = f32[8,4,64,64]{2,3,1,0:T(8,128)S(1)} fusion(f32[8,64,4,64]{1,3,2,0:T(8,128)S(1)} %fusion.1, f32[64]{0:T(128)S(1)} %iota_convert_fusion, f32[64]{0:T(128)S(1)} %add_multiply_fusion, pred[64]{0:T(512)(128)(4,1)S(1)} %broadcast_compare_fusion), kind=kOutput, calls=%fused_computation.24 | convolution fusion | flops 100683776 | bytes 1049152 | tf_op jit(solution)/shard_map/kn,akbl,lm->anbm/dot_general | solution.py:88
  142.0 2.1 %multiply_bitcast_fusion = (f32[8,64,4,64]{3,1,2,0:T(8,128)S(1)}, f32[8,64,4,64]{3,1,2,0:T(8,128)}) fusion(f32[8,4,64,64]{2,3,1,0:T(8,128)S(1)} %fusion.9, f32[64]{0:T(128)S(1)} %iota_convert_fusion, f32[64]{0:T(128)S(1)} %add_multiply_fusion, pred[64]{0:T(512)(128)(4,1)S(1)} %broadcast_compare_fusion), kind=kOutput, calls=%fused_computation.12 | convolution fusion | flops 100945920 | bytes 1573440 | tf_op jit(solution)/shard_map/kn,akbl,lm->anbm/dot_general | solution.py:88
  144.2 1.3 copy.41
  145.5 2.4 %mul.163 = f32[512,256]{0,1:T(8,128)} reshape(f32[8,64,4,64]{1,0,3,2:T(8,128)} %copy.41) | data formatting | bytes 1048576 | tf_op jit(solution)/shard_map/mul | solution.py:92
  147.9 2.1 %sub.7 = f32[512,256]{0,1:T(8,128)} subtract(f32[512,256]{0,1:T(8,128)} %copy.42, f32[512,256]{0,1:T(8,128)} %mul.163) | non-fusion elementwise | flops 131072 | bytes 1572864 | tf_op jit(solution)/shard_map/sub | solution.py:92
  149.9 2.0 %copy.44 = f32[512,256]{1,0:T(8,128)} copy(f32[512,256]{0,1:T(8,128)} %sub.7) | data formatting | bytes 1048576
  152.0 3.3 %fusion.12 = f32[8,4,64,64]{2,3,1,0:T(8,128)S(1)} fusion(f32[8,64,4,64]{1,3,2,0:T(8,128)S(1)} %copy-done.1, f32[64]{0:T(128)S(1)} %iota_convert_fusion, f32[64]{0:T(128)S(1)} %add_multiply_fusion, pred[64]{0:T(512)(128)(4,1)S(1)} %broadcast_compare_fusion), kind=kOutput, calls=%fused_computation.27 | convolution fusion | flops 100683776 | bytes 1049152 | tf_op jit(solution)/shard_map/kn,akbl,lm->anbm/dot_general | solution.py:80
  155.2 1.1 convolution_bitcast_fusion
  156.4 1.7 copy.35
  158.1 2.7 %reshape.58 = f32[512,256]{1,0:T(8,128)} reshape(f32[8,64,4,64]{3,2,1,0:T(4,128)} %copy.35) | data formatting | bytes 1048576 | tf_op jit(solution)/shard_map/reshape | solution.py:81
  160.8 1.9 %subtract_bitcast_fusion = f32[1,512,256]{2,1,0:T(8,128)} fusion(f32[512,256]{1,0:T(8,128)S(1)} %bitcast_add_fusion, f32[512,256]{1,0:T(8,128)} %reshape.58), kind=kLoop, calls=%fused_computation.17 | loop fusion | flops 131072 | bytes 1572864 | tf_op jit(solution)/shard_map/broadcast_in_dim | solution.py:81
  162.7 1.7 copy.52
  164.4 2.6 %reshape.64 = f32[512,256]{1,0:T(8,128)} reshape(f32[8,64,4,64]{3,2,1,0:T(4,128)} %copy.52) | data formatting | bytes 1048576
  (30 shorter events, 4.7 us)
Async XLA Ops:
  7.2 1.4 copy-start
  7.2 110.2 %reduce-scatter.2.cloned.1.call-start = ((), (), s32[]{:S(2)}) async-start(), calls=%async_computation.1 | async-start | bytes 4718592 | tf_op jit(solution)/shard_map/reduce_scatter | solution.py:64
  12.2 1.0 copy-start.3
  13.3 1.7 collective-permute-start
  15.2 24.1 %collective-permute-start.1 = (bf16[2,512,256]{2,1,0:T(8,128)(2,1)S(1)}, bf16[2,512,256]{2,1,0:T(8,128)(2,1)}, u32[]{:S(2)}, u32[]{:S(2)}) collective-permute-start(bf16[2,512,256]{2,1,0:T(8,128)(2,1)S(1)} %get-tuple-element.19), channel_id=1, source_target_pairs={{0,2},{1,3},{2,0},{3,1},{4,6},{5,7},{6,4},{7,5},{8,10},{9,11},{10,... | collective-permute-start | bytes 1572872 | tf_op jit(solution)/shard_map/ppermute | solution.py:30
  40.6 72.5 %collective-permute-start.2 = (bf16[4,512,256]{2,1,0:T(8,128)(2,1)S(1)}, bf16[4,512,256]{2,1,0:T(8,128)(2,1)}, u32[]{:S(2)}, u32[]{:S(2)}) collective-permute-start(bf16[4,512,256]{2,1,0:T(8,128)(2,1)S(1)} %bitcast.69), channel_id=1, source_target_pairs={{0,4},{1,5},{2,6},{3,7},{4,0},{5,1},{6,2},{7,3},{8,12},{9,13},{10,... | collective-permute-start | bytes 3145736 | tf_op jit(solution)/shard_map/ppermute | solution.py:30
  114.5 0.9 copy-start.5
  115.4 2.0 %copy-start.4 = (f32[1,512,256]{2,1,0:T(8,128)S(1)}, f32[1,512,256]{2,1,0:T(8,128)}, u32[]{:S(2)}) copy-start(f32[1,512,256]{2,1,0:T(8,128)} %param.8) | copy-start | bytes 1572868
  119.0 2.5 %copy-start.6 = (s32[64]{0:T(128)S(1)}, s32[64]{0:T(128)}, u32[]{:S(2)}) copy-start(s32[64]{0:T(128)} %param.9) | copy-start | bytes 772
  145.5 6.5 %copy-start.1 = (f32[8,64,4,64]{1,3,2,0:T(8,128)S(1)}, f32[8,64,4,64]{1,3,2,0:T(8,128)}, u32[]{:S(2)}) copy-start(f32[8,64,4,64]{1,3,2,0:T(8,128)} %fusion.54) | copy-start | bytes 1572868
  158.1 4.6 %copy-start.2 = (f32[8,64,4,64]{3,1,2,0:T(8,128)S(1)}, f32[8,64,4,64]{3,1,2,0:T(8,128)}, u32[]{:S(2)}) copy-start(f32[8,64,4,64]{3,1,2,0:T(8,128)} %get-tuple-element.17) | copy-start | bytes 1572868
Sparse Core Ops, SparseCore 0:
  12.3 83.0 reduce-scatter.1
